TPU v7x, 1024 devices: a whole 8x8x8 slice. The times are simulated.
1024 devices in a mesh: dp: 16 (over x, core), expert: 64 (over z, y).
Axes of the slice: x: 8, y: 8, z: 8, core: 2. Of those that a mesh axis runs over, the one named last changes fastest.
Arguments:
- tokens: bfloat16 [12288, 4096], P('expert', 'dp'), may hold values from -6 to 6
- routes: int32 [12288, 2], P('expert'), may hold values from 0 to 63, all different within a row; in each aligned block of 192 rows (0 to 191, 192 to 383, ...) at most 7 rows name the same one
- route_weight: float32 [12288, 2], P('expert'), may hold values from 0.2 to 1
- cotangent: bfloat16 [12288, 4096], P('expert', 'dp'), may hold values from -4 to 4
- w_in: bfloat16 [64, 4096, 2048], P('expert', 'dp'), may hold values from -0.09375 to 0.09375
- w_out: bfloat16 [64, 1024, 4096], P('expert', None, 'dp'), may hold values from -0.1875 to 0.1875
Outputs:
- mixed: bfloat16 [12288, 4096], P('expert', 'dp')
- grad_tokens: bfloat16 [12288, 4096], P('expert', 'dp')
- grad_in: bfloat16 [64, 4096, 2048], P('expert', 'dp')
- grad_out: bfloat16 [64, 1024, 4096], P('expert', None, 'dp')
Inputs may be any that keep to these rules, and one draw needn't show every extreme that they name: `routes`: each row names 2 different experts. Among the 192 rows of one index of the expert axis no expert is named more than 7 times, and in every draw some expert is named exactly 7 times by such a block.
All inputs are finite; a program needn't handle non-finite values.
Results may differ from a plain program's by a relative error of at most 0.0065.
Values may be sent and summed in bfloat16 or wider, within the bound.
A program may use at most 64 MiB of HBM per device.

v0:
```python
import jax
import jax.numpy as jnp
from jax import lax
from jax.sharding import PartitionSpec as P


def activate(pre_act, grad_hidden):
    units = pre_act.shape[1] // 2
    gate_part = pre_act[:, :units]
    up_part = pre_act[:, units:]
    sigmoid_gate = jax.nn.sigmoid(gate_part)
    silu_gate = gate_part * sigmoid_gate
    hidden = (silu_gate * up_part).astype(jnp.bfloat16)
    grad_gate = grad_hidden * up_part * sigmoid_gate * (1.0 + gate_part * (1.0 - sigmoid_gate))
    grad_up = grad_hidden * silu_gate
    return (hidden, jnp.concatenate([grad_gate, grad_up], axis=1).astype(jnp.bfloat16))


def per_device(tokens, routes, route_weight, cotangent, w_in, w_out):
    tok_rows, features = tokens.shape
    top_count = routes.shape[1]
    n_expert = lax.axis_size("expert")
    local_experts = w_in.shape[0]
    hidden_units = w_out.shape[1]
    experts = n_expert * local_experts
    capacity = tok_rows * top_count * 5 // (4 * experts)
    slot_count = experts * capacity
    flat_routes = routes.reshape(-1)
    onehot = (flat_routes[:, None] == jnp.arange(experts, dtype=jnp.int32)[None, :]).astype(
        jnp.int32
    )
    slot_rank = jnp.sum((jnp.cumsum(onehot, axis=0) - onehot) * onehot, axis=1)
    target = flat_routes * capacity + slot_rank
    placing = (target[None, :] == jnp.arange(slot_count, dtype=jnp.int32)[:, None]).astype(
        jnp.bfloat16
    )
    choose_token = jnp.sum(placing.reshape(slot_count, tok_rows, top_count), axis=2)
    scaled_grads = (route_weight[:, :, None] * cotangent[:, None, :].astype(jnp.float32)).astype(
        jnp.bfloat16
    )
    scaled_grads = scaled_grads.reshape(tok_rows * top_count, features)
    send_rows = jnp.dot(choose_token, tokens, preferred_element_type=jnp.float32).astype(
        jnp.bfloat16
    )
    send_grads = jnp.dot(placing, scaled_grads, preferred_element_type=jnp.float32).astype(
        jnp.bfloat16
    )
    send_rows = send_rows.reshape(n_expert, local_experts * capacity, features)
    send_grads = send_grads.reshape(n_expert, local_experts * capacity, features)
    routed_rows, routed_grads = (
        lax.all_to_all(send_rows, "expert", split_axis=0, concat_axis=0, tiled=True),
        lax.all_to_all(send_grads, "expert", split_axis=0, concat_axis=0, tiled=True),
    )
    rows_four = routed_rows.reshape(n_expert, local_experts, capacity, features)
    grads_four = routed_grads.reshape(n_expert, local_experts, capacity, features)
    total_rows = n_expert * local_experts * capacity
    pre_part = jnp.einsum("secd,edf->secf", rows_four, w_in, preferred_element_type=jnp.float32)
    back_part = jnp.einsum("secd,efd->secf", grads_four, w_out, preferred_element_type=jnp.float32)
    pre_flat = pre_part.reshape(total_rows, 2 * hidden_units)
    back_flat = back_part.reshape(total_rows, hidden_units)
    pre_share, back_share = (
        lax.psum_scatter(pre_flat, "dp", scatter_dimension=0, tiled=True),
        lax.psum_scatter(back_flat, "dp", scatter_dimension=0, tiled=True),
    )
    hidden_share, both_share = activate(pre_share, back_share)
    hidden, grad_both = (
        lax.all_gather(hidden_share, "dp", axis=0, tiled=True),
        lax.all_gather(both_share, "dp", axis=0, tiled=True),
    )
    hidden_four = hidden.reshape(n_expert, local_experts, capacity, hidden_units)
    both_four = grad_both.reshape(n_expert, local_experts, capacity, 2 * hidden_units)
    out_rows = jnp.einsum(
        "secf,efd->secd", hidden_four, w_out, preferred_element_type=jnp.float32
    ).astype(jnp.bfloat16)
    grad_rows = jnp.einsum(
        "secf,edf->secd", both_four, w_in, preferred_element_type=jnp.float32
    ).astype(jnp.bfloat16)
    grad_out = jnp.einsum(
        "secf,secd->efd", hidden_four, grads_four, preferred_element_type=jnp.float32
    ).astype(jnp.bfloat16)
    grad_in = jnp.einsum(
        "secd,secf->edf", rows_four, both_four, preferred_element_type=jnp.float32
    ).astype(jnp.bfloat16)
    home_out, home_grad = (
        lax.all_to_all(
            out_rows.reshape(n_expert, local_experts * capacity, features),
            "expert",
            split_axis=0,
            concat_axis=0,
            tiled=True,
        ),
        lax.all_to_all(
            grad_rows.reshape(n_expert, local_experts * capacity, features),
            "expert",
            split_axis=0,
            concat_axis=0,
            tiled=True,
        ),
    )
    route_out = jnp.dot(
        placing.T, home_out.reshape(slot_count, features), preferred_element_type=jnp.float32
    )
    route_out = route_out.reshape(tok_rows, top_count, features)
    mixed = jnp.sum(route_weight[:, :, None] * route_out, axis=1).astype(jnp.bfloat16)
    grad_tokens = jnp.dot(
        choose_token.T, home_grad.reshape(slot_count, features), preferred_element_type=jnp.float32
    )
    return (mixed, grad_tokens.astype(jnp.bfloat16), grad_in, grad_out)


def solution(mesh):
    placed = (
        P("expert", "dp"),
        P("expert", None),
        P("expert", None),
        P("expert", "dp"),
        P("expert", "dp", None),
        P("expert", None, "dp"),
    )
    return jax.shard_map(
        per_device,
        mesh=mesh,
        in_specs=placed,
        out_specs=(
            P("expert", "dp"),
            P("expert", "dp"),
            P("expert", "dp", None),
            P("expert", None, "dp"),
        ),
        check_vma=False,
    )
```

profile of v0, /device:TPU:1, one launch (start us, length us, event | category | flops | bytes accessed | tf_op | source)
XLA Modules:
  0.0 291.1 jit_solution(1484278208622366361)
XLA Ops:
  10.8 1.2 convolution_convert_fusion.2
  12.7 23.9 %all-to-all-start = ((bf16[64,7,256]{2,1,0:T(8,128)(2,1)}), bf16[64,7,256]{2,1,0:T(8,128)(2,1)S(1)}, u32[]{:S(2)}, u32[]{:S(2)}) async-start(bf16[64,7,256]{2,1,0:T(8,128)(2,1)} %reshape.135), calls=%async_computation | async-start | bytes 524288 | tf_op jit(solution)/shard_map/all_to_all | solution.py:51
  38.5 11.0 %all-to-all-done = bf16[64,7,256]{2,1,0:T(8,128)(2,1)S(1)} async-done(((bf16[64,7,256]{2,1,0:T(8,128)(2,1)}), bf16[64,7,256]{2,1,0:T(8,128)(2,1)S(1)}, u32[]{:S(2)}, u32[]{:S(2)}) %all-to-all-start) | async-done | bytes 229408 | tf_op jit(solution)/shard_map/all_to_all | solution.py:51
  49.5 5.7 %all-to-all-start.2 = ((bf16[64,7,256]{2,1,0:T(8,128)(2,1)}), bf16[64,7,256]{2,1,0:T(8,128)(2,1)S(1)}, u32[]{:S(2)}, u32[]{:S(2)}) async-start(bf16[64,7,256]{2,1,0:T(8,128)(2,1)} %reshape.141), calls=%async_computation.2 | async-start | bytes 524288 | tf_op jit(solution)/shard_map/all_to_all | solution.py:52
  55.9 4.1 %copy.74 = f32[64,1,7,2048]{3,2,0,1:T(8,128)} copy(f32[64,1,7,2048]{3,0,2,1:T(8,128)S(1)} %convolution_bitcast_fusion) | data formatting | bytes 7340032 | tf_op jit(solution)/shard_map/secd,edf->secf/transpose | solution.py:57
  60.0 4.8 %reshape.137 = f32[448,2048]{1,0:T(8,128)} reshape(f32[64,1,7,2048]{3,2,0,1:T(8,128)} %copy.74) | data formatting | bytes 7340032 | tf_op jit(solution)/shard_map/reshape | solution.py:59
  64.8 2.9 all-to-all-done.2
  70.0 1.6 reshape.142
  71.5 36.2 %fusion = f32[32,1024]{1,0:T(8,128)S(1)} fusion(f32[448,1024]{1,0:T(8,128)} %reshape.142), kind=kCustom, calls=%all-reduce-scatter | all-reduce-scatter fusion | flops 524289 | bytes 1970176
  107.7 3.1 %collective-permute-start = (f32[32,1024]{1,0:T(8,128)S(1)}, f32[32,1024]{1,0:T(8,128)S(1)}, u32[]{:S(2)}, u32[]{:S(2)}) collective-permute-start(f32[32,1024]{1,0:T(8,128)S(1)} %fusion), channel_id=1, source_target_pairs={{0,64},{64,128},{128,192},{192,256},{256,320},{320,384},{384,448},... | collective-permute-start | bytes 393224
  110.8 1.3 collective-permute-start.1
  112.1 1.4 fusion.35
  115.8 85.3 %all-reduce.5.cloned.1.call-done = f32[448,2048]{1,0:T(8,128)} async-done(((f32[448,2048]{1,0:T(8,128)}), f32[448,2048]{1,0:T(8,128)}) %all-reduce.5.cloned.1.call-update) | async-done | bytes 3670032
  202.8 20.3 %all-gather = bf16[16,28,1024]{2,1,0:T(8,128)(2,1)S(1)} all-gather(bf16[1,28,1024]{2,1,0:T(8,128)(2,1)S(1)} %get-tuple-element.6), channel_id=1, replica_groups=mesh['dp'=16,'expert'=64] {'dp'}, dimensions={0}, use_global_device_ids=true | all-gather | bytes 974848 | tf_op jit(solution)/shard_map/all_gather | solution.py:67
  223.5 2.2 convolution_convert_fusion.1
  226.5 12.3 %all-to-all-start.1 = ((bf16[64,7,256]{2,1,0:T(8,128)(2,1)}), bf16[64,7,256]{2,1,0:T(8,128)(2,1)S(1)}, u32[]{:S(2)}, u32[]{:S(2)}) async-start(bf16[64,7,256]{2,1,0:T(8,128)(2,1)} %copy.76), calls=%async_computation.1 | async-start | bytes 524288 | tf_op jit(solution)/shard_map/all_to_all | solution.py:85
  238.8 1.7 fusion.7
  240.6 11.7 %all-to-all-done.1 = bf16[64,7,256]{2,1,0:T(8,128)(2,1)S(1)} async-done(((bf16[64,7,256]{2,1,0:T(8,128)(2,1)}), bf16[64,7,256]{2,1,0:T(8,128)(2,1)S(1)}, u32[]{:S(2)}, u32[]{:S(2)}) %all-to-all-start.1) | async-done | bytes 229408 | tf_op jit(solution)/shard_map/all_to_all | solution.py:85
  253.0 2.6 reshape.143
  255.6 2.1 fusion.8
  258.6 10.6 %all-to-all-start.3 = ((bf16[64,7,256]{2,1,0:T(8,128)(2,1)}), bf16[64,7,256]{2,1,0:T(8,128)(2,1)}, u32[]{:S(2)}, u32[]{:S(2)}) async-start(bf16[64,7,256]{2,1,0:T(8,128)(2,1)} %copy.81), calls=%async_computation.3 | async-start | bytes 524288 | tf_op jit(solution)/shard_map/all_to_all | solution.py:92
  269.2 1.9 fusion.11
  271.1 4.3 %fusion.2 = bf16[1,256,2048]{2,1,0:T(8,128)(2,1)} fusion(bf16[64,7,2048]{2,1,0:T(8,128)(2,1)S(1)} %reshape.143, bf16[64,7,256]{2,1,0:T(8,128)(2,1)} %copy-done.3), kind=kOutput, calls=%fused_computation.3 | convolution fusion | flops 470286336 | bytes 3112960 | tf_op jit(solution)/shard_map/secd,secf->edf/dot_general | solution.py:81
  275.4 7.0 %all-to-all-done.3 = bf16[64,7,256]{2,1,0:T(8,128)(2,1)} async-done(((bf16[64,7,256]{2,1,0:T(8,128)(2,1)}), bf16[64,7,256]{2,1,0:T(8,128)(2,1)}, u32[]{:S(2)}, u32[]{:S(2)}) %all-to-all-start.3) | async-done | bytes 229408 | tf_op jit(solution)/shard_map/all_to_all | solution.py:92
  (54 shorter events, 16.5 us)
Async XLA Ops:
  7.2 48.1 %copy-start = (bf16[1,256,2048]{2,1,0:T(8,128)(2,1)S(1)}, bf16[1,256,2048]{2,1,0:T(8,128)(2,1)}, u32[]{:S(2)}) copy-start(bf16[1,256,2048]{2,1,0:T(8,128)(2,1)} %param.10) | copy-start | bytes 3145732
  7.2 29.5 %copy-start.5 = (bf16[192,256]{1,0:T(8,128)(2,1)S(1)}, bf16[192,256]{1,0:T(8,128)(2,1)}, u32[]{:S(2)}) copy-start(bf16[192,256]{1,0:T(8,128)(2,1)} %param.9) | copy-start | bytes 294916
  7.2 29.9 %copy-start.6 = (f32[192,2]{0,1:T(2,128)S(1)}, f32[192,2]{0,1:T(2,128)}, u32[]{:S(2)}) copy-start(f32[192,2]{0,1:T(2,128)} %param.8) | copy-start | bytes 4612
  12.7 36.8 %all-to-all-start = ((bf16[64,7,256]{2,1,0:T(8,128)(2,1)}), bf16[64,7,256]{2,1,0:T(8,128)(2,1)S(1)}, u32[]{:S(2)}, u32[]{:S(2)}) async-start(bf16[64,7,256]{2,1,0:T(8,128)(2,1)} %reshape.135), calls=%async_computation | async-start | bytes 524288 | tf_op jit(solution)/shard_map/all_to_all | solution.py:51
  49.5 6.4 %copy-start.3 = (bf16[64,7,256]{2,1,0:T(8,128)(2,1)}, bf16[64,7,256]{2,1,0:T(8,128)(2,1)S(1)}, u32[]{:S(2)}) copy-start(bf16[64,7,256]{2,1,0:T(8,128)(2,1)S(1)} %all-to-all-done) | copy-start | bytes 688132
  49.5 18.2 %all-to-all-start.2 = ((bf16[64,7,256]{2,1,0:T(8,128)(2,1)}), bf16[64,7,256]{2,1,0:T(8,128)(2,1)S(1)}, u32[]{:S(2)}, u32[]{:S(2)}) async-start(bf16[64,7,256]{2,1,0:T(8,128)(2,1)} %reshape.141), calls=%async_computation.2 | async-start | bytes 524288 | tf_op jit(solution)/shard_map/all_to_all | solution.py:52
  55.2 145.8 %all-reduce.5.cloned.1.call-start = ((), (), s32[]{:S(2)}) async-start(), calls=%async_computation.5 | async-start | bytes 7340032
  64.8 3.7 %copy-start.4 = (bf16[1,1024,256]{2,1,0:T(8,128)(2,1)S(1)}, bf16[1,1024,256]{2,1,0:T(8,128)(2,1)}, u32[]{:S(2)}) copy-start(bf16[1,1024,256]{2,1,0:T(8,128)(2,1)} %param.11) | copy-start | bytes 1572868
  64.8 188.2 %all-gather.4.cloned.1.call-start = ((), (), s32[]{:S(2)}) async-start(), calls=%async_computation.4 | async-start | bytes 2228224 | tf_op jit(solution)/shard_map/all_gather | solution.py:68
  67.7 0.7 copy-start.1
  107.7 7.7 %collective-permute-start = (f32[32,1024]{1,0:T(8,128)S(1)}, f32[32,1024]{1,0:T(8,128)S(1)}, u32[]{:S(2)}, u32[]{:S(2)}) collective-permute-start(f32[32,1024]{1,0:T(8,128)S(1)} %fusion), channel_id=1, source_target_pairs={{0,64},{64,128},{128,192},{192,256},{256,320},{320,384},{384,448},... | collective-permute-start | bytes 393224
  110.8 4.6 %collective-permute-start.1 = (f32[28,1024]{1,0:T(8,128)S(1)}, f32[28,1024]{1,0:T(8,128)S(1)}, u32[]{:S(2)}, u32[]{:S(2)}) collective-permute-start(f32[28,1024]{1,0:T(8,128)S(1)} %slice.17), channel_id=1, source_target_pairs={{0,128},{64,192},{128,256},{192,320},{256,384},{320,448},{384,512}... | collective-permute-start | bytes 344072
  223.5 15.3 %copy-start.2 = (bf16[64,7,256]{2,1,0:T(8,128)(2,1)S(1)}, bf16[64,7,256]{2,1,0:T(8,128)(2,1)}, u32[]{:S(2)}) copy-start(bf16[64,7,256]{2,1,0:T(8,128)(2,1)} %copy-done.1) | copy-start | bytes 688132
  226.5 25.7 %all-to-all-start.1 = ((bf16[64,7,256]{2,1,0:T(8,128)(2,1)}), bf16[64,7,256]{2,1,0:T(8,128)(2,1)S(1)}, u32[]{:S(2)}, u32[]{:S(2)}) async-start(bf16[64,7,256]{2,1,0:T(8,128)(2,1)} %copy.76), calls=%async_computation.1 | async-start | bytes 524288 | tf_op jit(solution)/shard_map/all_to_all | solution.py:85
  258.6 23.8 %all-to-all-start.3 = ((bf16[64,7,256]{2,1,0:T(8,128)(2,1)}), bf16[64,7,256]{2,1,0:T(8,128)(2,1)}, u32[]{:S(2)}, u32[]{:S(2)}) async-start(bf16[64,7,256]{2,1,0:T(8,128)(2,1)} %copy.81), calls=%async_computation.3 | async-start | bytes 524288 | tf_op jit(solution)/shard_map/all_to_all | solution.py:92
Sparse Core Ops, SparseCore 0:
  64.9 136.0 all-reduce.4
  203.7 45.7 all-gather.3
where the time goes:
time: 293 us; the launch traced here: 291 us
  waiting for transfers between devices  118 us (40%)
  starting transfers between devices  57 us (19%)
  blocking collectives  56.5 us (19%)
  local copies, waits for them, and re-layouts  24.1 us (8%)
  matrix products  15.7 us (5%)
  between operations  15.6 us (5%)
  other arithmetic  3.69 us (1%)
    unnamed x5, waiting for transfers between devices  85.9 us
    unnamed x1, blocking collectives  36.2 us
    all_to_all x1, starting transfers between devices, per_device(): lax.all_to_all(send_rows, 'expert', split_axis=0, concat_axis=0, tiled=True)  23.9 us
    all_gather x1, blocking collectives, per_device(): lax.all_gather(hidden_share, 'dp', axis=0, tiled=True)  20.3 us
    all_to_all x1, starting transfers between devices, per_device(): lax.all_to_all(out_rows.reshape(n_expert, local_experts * capacity, featu...  12.3 us
    all_to_all x1, waiting for transfers between devices, per_device(): lax.all_to_all(out_rows.reshape(n_expert, local_experts * capacity, featu...  11.7 us
    all_to_all x1, waiting for transfers between devices, per_device(): lax.all_to_all(send_rows, 'expert', split_axis=0, concat_axis=0, tiled=True)  11 us
    all_to_all x1, starting transfers between devices, per_device(): lax.all_to_all(grad_rows.reshape(n_expert, local_experts * capacity, feat...  10.6 us
  transfers between devices with their start and end apart: 8, of which 6 were waited for; matrix products, arithmetic and copies ran while one was open for 22% of the time, Pallas kernels for 0%

commit v1 on v0

v1 whole, which is shorter than its diff:
```python
import functools
import math

import jax
import jax.numpy as jnp
from jax import lax
from jax.experimental import pallas as pl
from jax.experimental.pallas import tpu as pltpu
from jax.sharding import PartitionSpec as P

BF = jnp.bfloat16
F32 = jnp.float32
MESH = pl.DeviceIdType.MESH
BLOCK = 16


def dot(a, b, dims=((1,), (0,))):
    return lax.dot_general(a, b, (dims, ((), ())), preferred_element_type=F32)


def ones_where(mask):
    return jnp.where(mask, 1.0, 0.0).astype(BF)


def iota(shape, dim):
    return lax.broadcasted_iota(jnp.int32, shape, dim)


def kernel(
    NX, NZ, NY, CAP,
    routes, weights, tokens, cot, w_in, w_out,
    mixed, grad_tokens, grad_in, grad_out,
    wi, wo, sa, sb, r1a, r1b, r2a, r2b, x, xp, pp, rsend, rrecv, g, acc, qmat, wcol,
    wsend, wrecv, wlocal, asend, arecv, alocal, xsend, xrecv, rs_s, rs_r, ag_s, ag_r, d_s, d_r,
):
    T, F = tokens.shape
    U = w_out.shape[0]
    E = NZ * NY
    UB = U // NX
    R = E * CAP
    HR = R // 2
    QR = R // 4
    K = NX // 2
    EG = E // 4
    HF = F // 2

    me_dp = lax.axis_index("dp")
    me_e = lax.axis_index("expert")
    xc, core = me_dp // 2, me_dp % 2
    Z, Y = me_e // NY, me_e % NY
    right = {"dp": ((xc + 1) % NX) * 2 + core, "expert": me_e}
    left = {"dp": ((xc + NX - 1) % NX) * 2 + core, "expert": me_e}
    partner = {"dp": xc * 2 + (1 - core), "expert": me_e}

    def z_peer(d):
        zz = (Z + d) % NZ
        return zz, {"dp": me_dp, "expert": zz * NY + Y}

    def y_peer(d):
        yy = (Y + d) % NY
        return yy, {"dp": me_dp, "expert": Z * NY + yy}

    def remote(src, dst, send, recv, device):
        return pltpu.make_async_remote_copy(
            src_ref=src, dst_ref=dst, send_sem=send, recv_sem=recv,
            device_id=device, device_id_type=MESH,
        )

    barrier = pltpu.get_barrier_semaphore()
    for d in range(1, NZ):
        pl.semaphore_signal(barrier, inc=1, device_id=z_peer(d)[1], device_id_type=MESH)
    for d in range(1, NY):
        pl.semaphore_signal(barrier, inc=1, device_id=y_peer(d)[1], device_id_type=MESH)
    for device in (right, left, partner):
        pl.semaphore_signal(barrier, inc=1, device_id=device, device_id_type=MESH)

    local_w = [
        pltpu.make_async_copy(w_in, wi.at[0], wlocal.at[0]),
        pltpu.make_async_copy(w_out, wo.at[0], wlocal.at[1]),
    ]
    for copy in local_w:
        copy.start()

    upper = ones_where(iota((T, T), 0) < iota((T, T), 1))
    diagonal = iota((T, T), 0) == iota((T, T), 1)
    named = [iota((E, T), 0) == routes[k : k + 1, :] for k in range(2)]
    before = dot(ones_where(named[0] | named[1]), upper)
    rows_of, cols_of, scaled, wcols = [], [], [], []
    cot_f = cot[...].astype(F32)
    for k in range(2):
        rank = jnp.sum(jnp.where(named[k], before, 0.0), axis=0, keepdims=True)
        place = routes[k : k + 1, :].astype(F32) * float(BLOCK) + rank
        col = jnp.sum(jnp.where(diagonal, place, 0.0), axis=1, keepdims=True)
        wc = jnp.sum(jnp.where(diagonal, weights[k : k + 1, :], 0.0), axis=1, keepdims=True)
        rows_of.append(place.astype(jnp.int32))
        cols_of.append(col.astype(jnp.int32))
        wcols.append(wc)
        scaled.append((wc * cot_f).astype(BF))
    token_rows = tokens[...]
    for i in range(4):
        ri = iota((EG * BLOCK, T), 0) + i * EG * BLOCK
        block = dot(ones_where((ri == rows_of[0]) | (ri == rows_of[1])), token_rows)
        for k in range(2):
            block += dot(ones_where(ri == rows_of[k] + 8), scaled[k])
        block = block.astype(BF)
        sa[0, i] = block[:, :HF]
        sb[0, i] = block[:, HF:]

    pl.semaphore_wait(barrier, NZ + NY + 1)

    def p1a(q, d):
        zz, device = z_peer(d)
        return remote(sa4(q, zz), r1a.at[q, Z], asend.at[q, 0, d], arecv.at[q, 0, d], device)

    def p1b(q, d):
        yy, device = y_peer(d)
        return remote(sb4(q, yy), r1b.at[q, Y], asend.at[q, 1, d], arecv.at[q, 1, d], device)

    def p2a(q, d):
        yy, device = y_peer(d)
        return remote(r1a.at[q, :, yy], r2a.at[q, :, Y], asend.at[q, 2, d], arecv.at[q, 2, d], device)

    def p2b(q, d):
        zz, device = z_peer(d)
        return remote(r1b.at[q, :, zz], r2b.at[q, Z], asend.at[q, 3, d], arecv.at[q, 3, d], device)

    def sa4(q, zz):
        return s4a.at[q, zz]

    def sb4(q, yy):
        return s4b.at[q, :, yy]

    s4a = sa.reshape(2, NZ, NY, BLOCK, HF)
    s4b = sb.reshape(2, NZ, NY, BLOCK, HF)

    def local(q, i):
        src, dst = (
            (sa4(q, Z), r1a.at[q, Z]),
            (sb4(q, Y), r1b.at[q, Y]),
            (r1a.at[q, :, Y], r2a.at[q, :, Y]),
            (r1b.at[q, :, Z], r2b.at[q, Z]),
        )[i]
        return pltpu.make_async_copy(src, dst, alocal.at[q, i])

    def order(n):
        ds = []
        for hop in range(n // 2, 0, -1):
            ds += [hop] if 2 * hop == n else [hop, n - hop]
        return ds

    def phase_one(q):
        for i in range(max(NZ, NY)):
            if i < len(order(NZ)):
                p1a(q, order(NZ)[i]).start()
            if i < len(order(NY)):
                p1b(q, order(NY)[i]).start()
        local(q, 0).start()
        local(q, 1).start()

    def phase_two(q):
        local(q, 0).wait()
        for d in order(NZ):
            p1a(q, d).wait_recv()
        for d in order(NY):
            p2a(q, d).start()
        local(q, 2).start()
        local(q, 1).wait()
        for d in order(NY):
            p1b(q, d).wait_recv()
        for d in order(NZ):
            p2b(q, d).start()
        local(q, 3).start()

    def phase_end(q):
        local(q, 2).wait()
        local(q, 3).wait()
        for d in order(NY):
            p2a(q, d).wait_recv()
        for d in order(NZ):
            p2b(q, d).wait_recv()

    phase_one(0)
    give_w = [
        remote(w_in, wi.at[1], wsend.at[0], wrecv.at[0], partner),
        remote(w_out, wo.at[1], wsend.at[1], wrecv.at[1], partner),
    ]
    for copy in give_w:
        copy.start()

    ci = iota((T, E * BLOCK), 1)
    for k in range(2):
        qmat[k] = ones_where(ci == cols_of[k])
        wcol[k] = jnp.broadcast_to(wcols[k], (T, F))
    qmat[2] = ones_where((ci == cols_of[0] + 8) | (ci == cols_of[1] + 8))

    phase_two(0)

    bj = iota((1, EG * BLOCK), 1)
    src, j = bj // BLOCK, bj % BLOCK
    pick = []
    for offset in (0, 8):
        ok = (j >= offset) & (j < offset + CAP)
        pick.append(jnp.where(ok, src * CAP + j - offset, -1))
    want = iota((QR, EG * BLOCK), 0)
    unpack = [ones_where(want == pick[a]) for a in range(2)]

    phase_end(0)
    for i in range(4):
        lo, hi = i * EG, (i + 1) * EG
        half_a = r2a[0].reshape(E, BLOCK, HF)[lo:hi].reshape(EG * BLOCK, HF)
        half_b = r2b[0].reshape(E, BLOCK, HF)[lo:hi].reshape(EG * BLOCK, HF)
        for a in range(2):
            x[i // 2, a, i % 2, :, :HF] = dot(unpack[a], half_a).astype(BF)
            x[i // 2, a, i % 2, :, HF:] = dot(unpack[a], half_b).astype(BF)
    give_x = remote(x.at[1 - core], xp, xsend, xrecv, partner)
    give_x.start()
    for copy in local_w:
        copy.wait()
    for copy in give_w:
        copy.wait_recv()
    give_x.wait_recv()

    def partial(jb):
        at = pl.multiple_of(jb * UB, UB)
        for n in range(3):
            total = None
            for v, rows in ((0, x.at[core]), (1, xp)):
                if n < 2:
                    lhs = rows[0].reshape(HR, F)
                    part = dot(lhs, wi[v, :, pl.ds(pl.multiple_of(n * U + at, UB), UB)])
                else:
                    lhs = rows[1].reshape(HR, F)
                    part = dot(lhs, wo[v, pl.ds(at, UB), :], ((1,), (1,)))
                total = part if total is None else total + part
            pp[jb, 0, :, n * UB : (n + 1) * UB] = total[:QR]
            pp[jb, 1, :, n * UB : (n + 1) * UB] = total[QR:]

    def chunk_of(direction, s):
        return (xc + K - s) % NX if direction == 0 else (xc + NX - K + s) % NX

    def ring(direction, s, q):
        return remote(
            rsend.at[direction, s, q], rrecv.at[direction, s, q],
            rs_s.at[direction, s, q], rs_r.at[direction, s, q],
            (right, left)[direction],
        )

    def exists(direction, s, q):
        return s > 0 or q == direction

    def ring_step(direction, s, q):
        value = pp[chunk_of(direction, s), q]
        if s > 0 and exists(direction, s - 1, q):
            ring(direction, s - 1, q).wait_recv()
            value = value + rrecv[direction, s - 1, q].astype(F32)
        rsend[direction, s, q] = value.astype(BF)
        ring(direction, s, q).start()

    partial((xc + K) % NX)
    for direction in range(2):
        ring_step(direction, 0, direction)
    if K > 1:
        partial(chunk_of(0, 1))
        ring_step(0, 1, 1)
        partial(chunk_of(1, 1))
        ring_step(1, 1, 0)

    def others(i, carry):
        partial((xc + NX - (K - 2) + i) % NX)
        return carry

    if K > 1:
        lax.fori_loop(0, 2 * (K - 2) + 1, others, 0)
    else:
        partial(xc)
    for s in range(1, K):
        for q_of in (1, 0):
            for direction in range(2):
                q = q_of if direction == 0 else 1 - q_of
                if s == 1 and q_of == 1:
                    continue
                ring_step(direction, s, q)

    def ag(direction, s, q):
        jb = (xc + NX - s) % NX if direction == 0 else (xc + s) % NX
        return remote(
            g.at[jb, core, q], g.at[jb, core, q],
            ag_s.at[direction, s, q], ag_r.at[direction, s, q],
            (right, left)[direction],
        )

    def across(jb, i, q):
        return remote(
            g.at[jb, core, q], g.at[jb, core, q], d_s.at[i, q], d_r.at[i, q], partner
        )

    for q in range(2):
        total = pp[xc, q]
        for direction in range(2):
            if exists(direction, K - 1, q):
                ring(direction, K - 1, q).wait_recv()
                total = total + rrecv[direction, K - 1, q].astype(F32)
        gate, up, gh = total[:, :UB], total[:, UB : 2 * UB], total[:, 2 * UB :]
        sg = jax.nn.sigmoid(gate)
        silu = gate * sg
        g[xc, core, q, :, :UB] = (silu * up).astype(BF)
        g[xc, core, q, :, UB : 2 * UB] = (gh * up * sg * (1.0 + gate * (1.0 - sg))).astype(BF)
        g[xc, core, q, :, 2 * UB :] = (gh * silu).astype(BF)
        for direction in range(2):
            if K > 1 or q == direction:
                ag(direction, 0, q).start()
        across(xc, 0, q).start()

    def ag_exists(direction, s, q):
        return s < K - 1 or (s == K - 1 and q == direction)

    crossed = [(xc, 0, q) for q in range(2)]
    for s in range(1, K + 1):
        for q_step in range(2):
            for direction in range(2):
                q = q_step if direction == 0 else 1 - q_step
                if not ag_exists(direction, s - 1, q):
                    continue
                ag(direction, s - 1, q).wait_recv()
                if s < K and ag_exists(direction, s, q):
                    ag(direction, s, q).start()
                jb = (xc + NX - s) % NX if direction == 0 else (xc + s) % NX
                i = s if direction == 0 or s == K else NX - s
                across(jb, i, q).start()
                crossed.append((jb, i, q))
    for args in crossed:
        across(*args).wait_recv()

    acc[...] = jnp.zeros_like(acc)

    def second(jb, carry):
        at = pl.multiple_of(jb * UB, UB)
        part = g[jb].reshape(R, 3 * UB)
        acc[0] += dot(part[:, :UB], wo[0, pl.ds(at, UB), :])
        acc[1] += dot(part[:, UB : 2 * UB], wi[0, :, pl.ds(at, UB)], ((1,), (1,))) + dot(
            part[:, 2 * UB :], wi[0, :, pl.ds(pl.multiple_of(U + at, UB), UB)], ((1,), (1,))
        )
        return carry

    lax.fori_loop(0, NX, second, 0)

    bi = iota((EG * BLOCK, 1), 0)
    src, j = bi // BLOCK, bi % BLOCK
    into = iota((EG * BLOCK, QR), 1)
    pack = []
    for offset in (0, 8):
        ok = (j >= offset) & (j < offset + CAP)
        pack.append(ones_where(into == jnp.where(ok, src * CAP + j - offset, -1)))
    for i in range(4):
        block = dot(pack[0], acc[0, i * QR : (i + 1) * QR].astype(BF)) + dot(
            pack[1], acc[1, i * QR : (i + 1) * QR].astype(BF)
        )
        block = block.astype(BF)
        sa[1, i] = block[:, :HF]
        sb[1, i] = block[:, HF:]
    phase_one(1)

    rows_all = jnp.concatenate([x[h, 0].reshape(HR, F) for h in range(2)], axis=0)
    grads_all = jnp.concatenate([x[h, 1].reshape(HR, F) for h in range(2)], axis=0)

    def weight_grads(jb, carry):
        at = pl.multiple_of(jb * UB, UB)
        part = g[jb].reshape(R, 3 * UB)
        for n in range(2):
            grad_in[:, pl.ds(pl.multiple_of(n * U + at, UB), UB)] = dot(
                rows_all, part[:, (n + 1) * UB : (n + 2) * UB], ((0,), (0,))
            ).astype(BF)
        grad_out[pl.ds(at, UB), :] = dot(part[:, :UB], grads_all, ((0,), (0,))).astype(BF)
        return carry

    lax.fori_loop(0, NX // 2, weight_grads, 0)
    phase_two(1)
    lax.fori_loop(NX // 2, NX, weight_grads, 0)
    phase_end(1)

    home = jnp.concatenate(
        [r2a[1].reshape(E * BLOCK, HF), r2b[1].reshape(E * BLOCK, HF)], axis=1
    )
    mixed[...] = (wcol[0] * dot(qmat[0], home) + wcol[1] * dot(qmat[1], home)).astype(BF)
    grad_tokens[...] = dot(qmat[2], home).astype(BF)

    for copy in give_w + [give_x]:
        copy.wait_send()
    for q in range(2):
        for d in order(NZ):
            p1a(q, d).wait_send()
            p2b(q, d).wait_send()
        for d in order(NY):
            p1b(q, d).wait_send()
            p2a(q, d).wait_send()
    for direction in range(2):
        for s in range(K):
            for q in range(2):
                if exists(direction, s, q):
                    ring(direction, s, q).wait_send()
                if ag_exists(direction, s, q):
                    ag(direction, s, q).wait_send()
    for args in crossed:
        across(*args).wait_send()


def per_device(tokens, routes, route_weight, cotangent, w_in, w_out):
    T, F = tokens.shape
    E = lax.axis_size("expert")
    NX = lax.axis_size("dp") // 2
    NY = 1 << (int(math.log2(E)) // 2)
    NZ = E // NY
    U = w_out.shape[1]
    CAP = T * 2 * 5 // (4 * E)
    UB, R = U // NX, E * CAP
    HR, QR, K, HF = R // 2, R // 4, NX // 2, F // 2
    EG = E // 4
    dma = pltpu.SemaphoreType.DMA
    far = max(NZ, NY)
    vmem = pl.BlockSpec(memory_space=pltpu.VMEM)
    anywhere = pl.BlockSpec(memory_space=pl.ANY)
    mixed, grad_tokens, grad_in, grad_out = pl.pallas_call(
        functools.partial(kernel, NX, NZ, NY, CAP),
        out_shape=(
            jax.ShapeDtypeStruct((T, F), BF),
            jax.ShapeDtypeStruct((T, F), BF),
            jax.ShapeDtypeStruct((F, 2 * U), BF),
            jax.ShapeDtypeStruct((U, F), BF),
        ),
        in_specs=[vmem] * 4 + [anywhere] * 2,
        out_specs=(vmem,) * 4,
        scratch_shapes=[
            pltpu.VMEM((2, F, 2 * U), BF),
            pltpu.VMEM((2, U, F), BF),
            pltpu.VMEM((2, 4, EG * BLOCK, HF), BF),
            pltpu.VMEM((2, 4, EG * BLOCK, HF), BF),
            pltpu.VMEM((2, NZ, NY, BLOCK, HF), BF),
            pltpu.VMEM((2, NY, NZ, BLOCK, HF), BF),
            pltpu.VMEM((2, NZ, NY, BLOCK, HF), BF),
            pltpu.VMEM((2, NZ, NY, BLOCK, HF), BF),
            pltpu.VMEM((2, 2, 2, QR, F), BF),
            pltpu.VMEM((2, 2, QR, F), BF),
            pltpu.VMEM((NX, 2, QR, 3 * UB), F32),
            pltpu.VMEM((2, K, 2, QR, 3 * UB), BF),
            pltpu.VMEM((2, K, 2, QR, 3 * UB), BF),
            pltpu.VMEM((NX, 2, 2, QR, 3 * UB), BF),
            pltpu.VMEM((2, R, F), F32),
            pltpu.VMEM((3, T, E * BLOCK), BF),
            pltpu.VMEM((2, T, F), F32),
            dma((2,)), dma((2,)), dma((2,)),
            dma((2, 4, far)), dma((2, 4, far)), dma((2, 4)),
            dma, dma,
            dma((2, K, 2)), dma((2, K, 2)),
            dma((2, K, 2)), dma((2, K, 2)),
            dma((NX, 2)), dma((NX, 2)),
        ],
        compiler_params=pltpu.CompilerParams(
            collective_id=0, has_side_effects=True, vmem_limit_bytes=50 * 1024 * 1024
        ),
    )(routes.T, route_weight.T, tokens, cotangent, w_in[0], w_out[0])
    return mixed, grad_tokens, grad_in[None], grad_out[None]


def solution(mesh):
    placed = (
        P("expert", "dp"),
        P("expert", None),
        P("expert", None),
        P("expert", "dp"),
        P("expert", "dp", None),
        P("expert", None, "dp"),
    )
    return jax.shard_map(
        per_device,
        mesh=mesh,
        in_specs=placed,
        out_specs=(
            P("expert", "dp"),
            P("expert", "dp"),
            P("expert", "dp", None),
            P("expert", None, "dp"),
        ),
        check_vma=False,
    )
```

time: 293 us -> 104 us (0.35)
  waiting for transfers between devices: 118 us -> 0 us
  Pallas kernels: 0 us -> 94.9 us
  starting transfers between devices: 57 us -> 0 us
  blocking collectives: 56.5 us -> 0 us
  local copies, waits for them, and re-layouts: 24.1 us -> 7.78 us
  matrix products: 15.7 us -> 0 us
  between operations: 15.6 us -> 0.66 us
  other arithmetic: 3.69 us -> 0 us
    pallas_call x0 -> x1, Pallas kernels: none -> 94.9 us  [per_device(): pl.pallas_call(functools.partial(kernel, NX, NZ, NY, CAP), out_shape=(jax...]
    unnamed x5 -> x0, waiting for transfers between devices: 85.9 us -> none
    all_to_all x4 -> x0, starting transfers between devices: 52.5 us -> none  [the longest x1 23.9 us: per_device(): lax.all_to_all(send_rows, 'expert', split_axis=0, concat_axis=0, tiled=True)]
    unnamed x1 -> x0, blocking collectives: 36.2 us -> none
    all_to_all x4 -> x0, waiting for transfers between devices: 32.5 us -> none  [the longest x1 11.7 us: per_device(): lax.all_to_all(out_rows.reshape(n_expert, local_experts * capacity, featu...]
    all_gather x1 -> x0, blocking collectives: 20.3 us -> none  [per_device(): lax.all_gather(hidden_share, 'dp', axis=0, tiled=True)]
    dot_general x10 -> x0, matrix products: 15.7 us -> none  [the longest x1 4.27 us: per_device(): jnp.einsum('secd,secf->edf', rows_four, both_four, preferred_element_type...]
    reshape x7 -> x0, local copies, waits for them, and re-layouts: 9.83 us -> none  [the longest x1 4.75 us: per_device(): pre_flat = pre_part.reshape(total_rows, 2 * hidden_units)]
  transfers between devices with their start and end apart: 8 -> 0, of which waited for: 6 -> 0; matrix products, arithmetic and copies ran while one was open for 22% -> 0% of each run, Pallas kernels for 0% -> 0%
where the time goes in v1:
time: 104 us; the launch traced here: 103 us
  Pallas kernels  94.9 us (91%)
  local copies, waits for them, and re-layouts  7.78 us (7%)
    pallas_call x1, Pallas kernels, per_device(): pl.pallas_call(functools.partial(kernel, NX, NZ, NY, CAP), out_shape=(jax...  94.9 us
    unnamed x16, local copies, waits for them, and re-layouts  7.78 us

profile of v1, /device:TPU:1, one launch (start us, length us, event | category | flops | bytes accessed | tf_op | source)
XLA Modules:
  0.0 103.3 jit_solution(4350136349230848524)
XLA Ops:
  0.6 0.0 copy-start.5
  0.6 0.0 copy-start.4
  0.7 0.7 copy-done.5
  1.3 0.0 copy-done.4
  1.3 0.0 copy-start
  1.3 1.2 %copy-done = bf16[1,256,2048]{2,1,0:T(8,128)(2,1)S(1)} copy-done((bf16[1,256,2048]{2,1,0:T(8,128)(2,1)S(1)}, bf16[1,256,2048]{2,1,0:T(8,128)(2,1)}, u32[]{:S(2)}) %copy-start) | copy-done | bytes 1048600
  2.6 0.0 copy-start.1
  2.6 1.0 %copy-done.1 = bf16[1,1024,256]{2,1,0:T(8,128)(2,1)S(1)} copy-done((bf16[1,1024,256]{2,1,0:T(8,128)(2,1)S(1)}, bf16[1,1024,256]{2,1,0:T(8,128)(2,1)}, u32[]{:S(2)}) %copy-start.1) | copy-done | bytes 524312
  3.6 0.0 copy-start.2
  3.6 0.9 copy-done.2
  4.5 0.0 copy-start.3
  4.5 0.9 copy-done.3
  5.4 94.9 %shard_map.93 = (bf16[192,256]{1,0:T(8,128)(2,1)S(1)}, bf16[192,256]{1,0:T(8,128)(2,1)S(1)}, bf16[256,2048]{1,0:T(8,128)(2,1)S(1)}, bf16[1024,256]{1,0:T(8,128)(2,1)S(1)}) custom-call(s32[2,192]{1,0:T(2,128)S(1)} %bitcast.10, f32[2,192]{1,0:T(2,128)S(1)} %bitcast.11, bf16[192,256]{1,0:T(8,128)(2,1)S(1)} %copy-done.2, bf16[192,256]{1,0:T(8,128)(2,1)S(1)} %copy-done.3, ...), custom_call_target="tpu_custom_call" | custom-call | tf_op jit(solution)/shard_map/pallas_call | solution.py:422
  100.3 0.6 copy.14
  100.9 0.6 copy.15
  101.6 1.0 copy.16
  102.5 0.8 copy.17
Async XLA Ops:
  0.6 0.7 copy-start.5
  0.6 0.7 copy-start.4
  1.3 1.2 %copy-start = (bf16[1,256,2048]{2,1,0:T(8,128)(2,1)S(1)}, bf16[1,256,2048]{2,1,0:T(8,128)(2,1)}, u32[]{:S(2)}) copy-start(bf16[1,256,2048]{2,1,0:T(8,128)(2,1)} %param.10) | copy-start | bytes 3145732
  2.6 1.0 %copy-start.1 = (bf16[1,1024,256]{2,1,0:T(8,128)(2,1)S(1)}, bf16[1,1024,256]{2,1,0:T(8,128)(2,1)}, u32[]{:S(2)}) copy-start(bf16[1,1024,256]{2,1,0:T(8,128)(2,1)} %param.11) | copy-start | bytes 1572868
  3.6 0.9 copy-start.2
  4.5 0.9 copy-start.3

commit v2 on v0

v2 whole, which is shorter than its diff:
```python
import functools
import math

import jax
import jax.numpy as jnp
from jax import lax
from jax.experimental import pallas as pl
from jax.experimental.pallas import tpu as pltpu
from jax.sharding import PartitionSpec as P

BF = jnp.bfloat16
F32 = jnp.float32
MESH = pl.DeviceIdType.MESH
BLOCK = 8
HALF = 4


def dot(a, b, dims=((1,), (0,))):
    return lax.dot_general(a, b, (dims, ((), ())), preferred_element_type=F32)


def ones_where(mask):
    return jnp.where(mask, 1.0, 0.0).astype(BF)


def iota(shape, dim):
    return lax.broadcasted_iota(jnp.int32, shape, dim)


def kernel(
    NX, NZ, NY, CAP,
    routes_h, weights_h, tokens_h, cot_h, w_in, w_out,
    mixed, grad_tokens, grad_in, grad_out,
    routes, weights, tokens, cot, wi, wo, sa, sb, r1a, r1b, r2a, r2b, qmat, wcol,
    x0, xp0, pp0, rsend0, rrecv0, g0, acc0,
    x1, xp1, pp1, rsend1, rrecv1, g1, acc1,
    isem, wsend, wrecv, wlocal, asend, arecv, alocal, xsend, xrecv,
    rs_s, rs_r, ag_s, ag_r, d_s, d_r,
):
    T, F = tokens_h.shape
    U = w_out.shape[0]
    E = NZ * NY
    UB = U // NX
    K = NX // 2
    EG = E // 4
    HF = F // 2
    groups = ((0, (CAP + 1) // 2), ((CAP + 1) // 2, CAP // 2))
    x, xp, pp, rsend, rrecv = (x0, x1), (xp0, xp1), (pp0, pp1), (rsend0, rsend1), (rrecv0, rrecv1)
    g, acc = (g0, g1), (acc0, acc1)

    me_dp = lax.axis_index("dp")
    me_e = lax.axis_index("expert")
    xc, core = me_dp // 2, me_dp % 2
    Z, Y = me_e // NY, me_e % NY
    right = {"dp": ((xc + 1) % NX) * 2 + core, "expert": me_e}
    left = {"dp": ((xc + NX - 1) % NX) * 2 + core, "expert": me_e}
    partner = {"dp": xc * 2 + (1 - core), "expert": me_e}

    def z_peer(d):
        zz = (Z + d) % NZ
        return zz, {"dp": me_dp, "expert": zz * NY + Y}

    def y_peer(d):
        yy = (Y + d) % NY
        return yy, {"dp": me_dp, "expert": Z * NY + yy}

    def remote(src, dst, send, recv, device):
        return pltpu.make_async_remote_copy(
            src_ref=src, dst_ref=dst, send_sem=send, recv_sem=recv,
            device_id=device, device_id_type=MESH,
        )

    given = [
        pltpu.make_async_copy(src, dst, isem.at[i])
        for i, (src, dst) in enumerate(
            ((routes_h, routes), (weights_h, weights), (cot_h, cot), (tokens_h, tokens))
        )
    ]
    for copy in given:
        copy.start()
    barrier = pltpu.get_barrier_semaphore()
    for d in range(1, NZ):
        pl.semaphore_signal(barrier, inc=1, device_id=z_peer(d)[1], device_id_type=MESH)
    for d in range(1, NY):
        pl.semaphore_signal(barrier, inc=1, device_id=y_peer(d)[1], device_id_type=MESH)
    for device in (right, left, partner):
        pl.semaphore_signal(barrier, inc=1, device_id=device, device_id_type=MESH)

    local_w = [
        pltpu.make_async_copy(w_in, wi.at[0], wlocal.at[0]),
        pltpu.make_async_copy(w_out, wo.at[0], wlocal.at[1]),
    ]
    for copy in local_w:
        copy.start()

    upper = ones_where(iota((T, T), 0) < iota((T, T), 1))
    diagonal = iota((T, T), 0) == iota((T, T), 1)

    def slots(expert, rank, group):
        first, count = groups[group]
        inside = (rank >= first) & (rank < first + count)
        return jnp.where(inside, expert * BLOCK + rank - first, -2 * BLOCK)

    given[0].wait()
    named = [iota((E, T), 0) == routes[k : k + 1, :] for k in range(2)]
    before = dot(ones_where(named[0] | named[1]), upper)
    for copy in given[1:]:
        copy.wait()
    cot_f = cot[...].astype(F32)
    rows_of, cols_of, scaled, wcols = [], [], [], []
    for k in range(2):
        rank = jnp.sum(jnp.where(named[k], before, 0.0), axis=0, keepdims=True)
        place = routes[k : k + 1, :].astype(F32) * 16.0 + rank
        col = jnp.sum(jnp.where(diagonal, place, 0.0), axis=1, keepdims=True).astype(jnp.int32)
        wc = jnp.sum(jnp.where(diagonal, weights[k : k + 1, :], 0.0), axis=1, keepdims=True)
        rank_i = rank.astype(jnp.int32)
        rows_of.append([slots(routes[k : k + 1, :], rank_i, n) for n in range(2)])
        cols_of.append([slots(col // 16, col % 16, n) for n in range(2)])
        wcols.append(wc)
        scaled.append((wc * cot_f).astype(BF))
    token_rows = tokens[...]

    flat_sa, flat_sb = sa.reshape(2, 2, E * BLOCK, HF), sb.reshape(2, 2, E * BLOCK, HF)
    flat_ra, flat_rb = r2a.reshape(2, 2, E * BLOCK, HF), r2b.reshape(2, 2, E * BLOCK, HF)
    BR = EG * BLOCK

    def build(n):
        for i in range(2):
            ri = iota((2 * BR, T), 0) + i * 2 * BR
            a, b = rows_of[0][n], rows_of[1][n]
            block = dot(ones_where((ri == a) | (ri == b)), token_rows)
            for k in range(2):
                block += dot(ones_where(ri == rows_of[k][n] + HALF), scaled[k])
            block = block.astype(BF)
            flat_sa[0, n, 2 * i * BR : 2 * (i + 1) * BR] = block[:, :HF]
            flat_sb[0, n, 2 * i * BR : 2 * (i + 1) * BR] = block[:, HF:]

    def p1a(q, n, d):
        zz, device = z_peer(d)
        return remote(sa.at[q, n, zz], r1a.at[q, n, Z], asend.at[q, n, 0, d], arecv.at[q, n, 0, d], device)

    def p1b(q, n, d):
        yy, device = y_peer(d)
        return remote(sb.at[q, n, :, yy], r1b.at[q, n, Y], asend.at[q, n, 1, d], arecv.at[q, n, 1, d], device)

    def p2a(q, n, d):
        yy, device = y_peer(d)
        return remote(r1a.at[q, n, :, yy], r2a.at[q, n, :, Y], asend.at[q, n, 2, d], arecv.at[q, n, 2, d], device)

    def p2b(q, n, d):
        zz, device = z_peer(d)
        return remote(r1b.at[q, n, :, zz], r2b.at[q, n, Z], asend.at[q, n, 3, d], arecv.at[q, n, 3, d], device)

    def local(q, n, i):
        src, dst = (
            (sa.at[q, n, Z], r1a.at[q, n, Z]),
            (sb.at[q, n, :, Y], r1b.at[q, n, Y]),
            (r1a.at[q, n, :, Y], r2a.at[q, n, :, Y]),
            (r1b.at[q, n, :, Z], r2b.at[q, n, Z]),
        )[i]
        return pltpu.make_async_copy(src, dst, alocal.at[q, n, i])

    def order(size):
        ds = []
        for hop in range(size // 2, 0, -1):
            ds += [hop] if 2 * hop == size else [hop, size - hop]
        return ds

    def phase_one(q, n):
        for i in range(max(NZ, NY)):
            if i < len(order(NZ)):
                p1a(q, n, order(NZ)[i]).start()
            if i < len(order(NY)):
                p1b(q, n, order(NY)[i]).start()
        local(q, n, 0).start()
        local(q, n, 1).start()

    def phase_two(q, n):
        local(q, n, 0).wait()
        for d in order(NZ):
            p1a(q, n, d).wait_recv()
        for d in order(NY):
            p2a(q, n, d).start()
        local(q, n, 2).start()
        local(q, n, 1).wait()
        for d in order(NY):
            p1b(q, n, d).wait_recv()
        for d in order(NZ):
            p2b(q, n, d).start()
        local(q, n, 3).start()

    def phase_end(q, n):
        local(q, n, 2).wait()
        local(q, n, 3).wait()
        for d in order(NY):
            p2a(q, n, d).wait_recv()
        for d in order(NZ):
            p2b(q, n, d).wait_recv()

    def unpack(n):
        count = groups[n][1]
        QR = EG * count
        bj = iota((1, BR), 1)
        src, j = bj // BLOCK, bj % BLOCK
        want = iota((QR, BR), 0)
        for a in range(2):
            ok = (j >= a * HALF) & (j < a * HALF + count)
            pick = ones_where(want == jnp.where(ok, src * count + j - a * HALF, -1))
            for i in range(4):
                lo, hi = i * BR, (i + 1) * BR
                x[n][i // 2, a, i % 2, :, :HF] = dot(pick, flat_ra[0, n, lo:hi]).astype(BF)
                x[n][i // 2, a, i % 2, :, HF:] = dot(pick, flat_rb[0, n, lo:hi]).astype(BF)

    def give_x(n):
        return remote(x[n].at[1 - core], xp[n], xsend.at[n], xrecv.at[n], partner)

    def partial(n, jb):
        QR = EG * groups[n][1]
        HR = 2 * QR
        at = pl.multiple_of(jb * UB, UB)
        total, below = None, None
        for v, rows in ((0, x[n].at[core]), (1, xp[n])):
            both = jnp.concatenate(
                [wi[v, :, pl.ds(at, UB)], wi[v, :, pl.ds(pl.multiple_of(U + at, UB), UB)]], axis=1
            )
            part = dot(rows[0].reshape(HR, F), both)
            back = dot(rows[1].reshape(HR, F), wo[v, pl.ds(at, UB), :], ((1,), (1,)))
            total = part if v == 0 else total + part
            below = back if v == 0 else below + back
        for q in range(2):
            pp[n][jb, q, :, : 2 * UB] = total[q * QR : (q + 1) * QR]
            pp[n][jb, q, :, 2 * UB :] = below[q * QR : (q + 1) * QR]

    def chunk_of(direction, s):
        return (xc + K - s) % NX if direction == 0 else (xc + NX - K + s) % NX

    def ring(n, direction, s, q):
        return remote(
            rsend[n].at[direction, s, q], rrecv[n].at[direction, s, q],
            rs_s.at[n, direction, s, q], rs_r.at[n, direction, s, q],
            (right, left)[direction],
        )

    def exists(direction, s, q):
        return s > 0 or q == direction

    def ring_step(n, direction, s, q):
        value = pp[n][chunk_of(direction, s), q]
        if s > 0 and exists(direction, s - 1, q):
            ring(n, direction, s - 1, q).wait_recv()
            value = value + rrecv[n][direction, s - 1, q].astype(F32)
        rsend[n][direction, s, q] = value.astype(BF)
        ring(n, direction, s, q).start()

    def ring_first(n):
        partial(n, (xc + K) % NX)
        for direction in range(2):
            ring_step(n, direction, 0, direction)
        if K > 1:
            for direction in range(2):
                partial(n, chunk_of(direction, 1))
                ring_step(n, direction, 1, 1 - direction)
        else:
            partial(n, xc)

    def ring_ahead(n, s):
        if s < K:
            for direction in range(2):
                partial(n, chunk_of(direction, s))
        elif s == K:
            partial(n, xc)

    def ring_round(n, s):
        if s >= K:
            return
        for far in (1, 0):
            for direction in range(2):
                if not (s == 1 and far == 1):
                    ring_step(n, direction, s, far if direction == 0 else 1 - far)
        ring_ahead(n, s + 1)

    def ag(n, direction, s, q):
        jb = (xc + NX - s) % NX if direction == 0 else (xc + s) % NX
        return remote(
            g[n].at[jb, core, q], g[n].at[jb, core, q],
            ag_s.at[n, direction, s, q], ag_r.at[n, direction, s, q],
            (right, left)[direction],
        )

    def across(n, jb, i, q):
        return remote(
            g[n].at[jb, core, q], g[n].at[jb, core, q], d_s.at[n, i, q], d_r.at[n, i, q], partner
        )

    def ag_exists(direction, s, q):
        return s < K - 1 or (s == K - 1 and q == direction)

    crossed = ([], [])

    def activate(n):
        for q in range(2):
            total = pp[n][xc, q]
            for direction in range(2):
                if exists(direction, K - 1, q):
                    ring(n, direction, K - 1, q).wait_recv()
                    total = total + rrecv[n][direction, K - 1, q].astype(F32)
            gate, up, gh = total[:, :UB], total[:, UB : 2 * UB], total[:, 2 * UB :]
            sg = jax.nn.sigmoid(gate)
            silu = gate * sg
            g[n][xc, core, q, :, :UB] = (silu * up).astype(BF)
            g[n][xc, core, q, :, UB : 2 * UB] = (gh * up * sg * (1.0 + gate * (1.0 - sg))).astype(BF)
            g[n][xc, core, q, :, 2 * UB :] = (gh * silu).astype(BF)
            for direction in range(2):
                if ag_exists(direction, 0, q):
                    ag(n, direction, 0, q).start()
            across(n, xc, 0, q).start()
            crossed[n].append((n, xc, 0, q))

    def gather_round(n, s):
        if s > K:
            return
        for q_step in range(2):
            for direction in range(2):
                q = q_step if direction == 0 else 1 - q_step
                if not ag_exists(direction, s - 1, q):
                    continue
                ag(n, direction, s - 1, q).wait_recv()
                if s < K and ag_exists(direction, s, q):
                    ag(n, direction, s, q).start()
                jb = (xc + NX - s) % NX if direction == 0 else (xc + s) % NX
                i = s if direction == 0 or s == K else NX - s
                across(n, jb, i, q).start()
                crossed[n].append((n, jb, i, q))

    def second(n, s):
        R = E * groups[n][1]
        todo = [args for args in crossed[n] if args[2] == s or args[2] == NX - s]
        for args in todo:
            across(*args).wait_recv()
        for jb in [args[1] for args in todo if args[3] == 0]:
            at = pl.multiple_of(jb * UB, UB)
            part = g[n][jb].reshape(R, 3 * UB)
            both = jnp.concatenate(
                [wi[0, :, pl.ds(at, UB)], wi[0, :, pl.ds(pl.multiple_of(U + at, UB), UB)]], axis=1
            )
            down = dot(part[:, :UB], wo[0, pl.ds(at, UB), :])
            back = dot(part[:, UB:], both, ((1,), (1,)))
            if s == 0:
                acc[n][0] = down
                acc[n][1] = back
            else:
                acc[n][0] += down
                acc[n][1] += back

    def pack(n):
        count = groups[n][1]
        QR = EG * count
        bi = iota((BR, 1), 0)
        src, j = bi // BLOCK, bi % BLOCK
        into = iota((BR, QR), 1)
        puts = []
        for a in range(2):
            ok = (j >= a * HALF) & (j < a * HALF + count)
            puts.append(ones_where(into == jnp.where(ok, src * count + j - a * HALF, -1)))
        for i in range(4):
            rows = slice(i * QR, (i + 1) * QR)
            block = dot(puts[0], acc[n][0, rows].astype(BF)) + dot(puts[1], acc[n][1, rows].astype(BF))
            block = block.astype(BF)
            flat_sa[1, n, i * BR : (i + 1) * BR] = block[:, :HF]
            flat_sb[1, n, i * BR : (i + 1) * BR] = block[:, HF:]

    def way_back(n):
        second(n, K)
        pack(n)
        phase_one(1, n)

    def weight_grads(jb, carry):
        at = pl.multiple_of(jb * UB, UB)
        ups, downs = [None, None], None
        for n in range(2):
            R = E * groups[n][1]
            part = g[n][jb].reshape(R, 3 * UB)
            rows = jnp.concatenate([x[n][h, 0].reshape(R // 2, F) for h in range(2)], axis=0)
            grads = jnp.concatenate([x[n][h, 1].reshape(R // 2, F) for h in range(2)], axis=0)
            for m in range(2):
                term = dot(rows, part[:, (m + 1) * UB : (m + 2) * UB], ((0,), (0,)))
                ups[m] = term if n == 0 else ups[m] + term
            term = dot(part[:, :UB], grads, ((0,), (0,)))
            downs = term if n == 0 else downs + term
        for m in range(2):
            grad_in[:, pl.ds(pl.multiple_of(m * U + at, UB), UB)] = ups[m].astype(BF)
        grad_out[pl.ds(at, UB), :] = downs.astype(BF)
        return carry

    build(0)
    pl.semaphore_wait(barrier, NZ + NY + 1)
    phase_one(0, 0)
    give_w = [
        remote(w_in, wi.at[1], wsend.at[0], wrecv.at[0], partner),
        remote(w_out, wo.at[1], wsend.at[1], wrecv.at[1], partner),
    ]
    for copy in give_w:
        copy.start()
    build(1)
    phase_two(0, 0)
    phase_one(0, 1)
    for k in range(2):
        wcol[k] = jnp.broadcast_to(wcols[k], (T, F))
    ci = iota((T, E * BLOCK), 1)
    for n in range(2):
        for k in range(2):
            qmat[n, k] = ones_where(ci == cols_of[k][n])
        qmat[n, 2] = ones_where((ci == cols_of[0][n] + HALF) | (ci == cols_of[1][n] + HALF))
    phase_end(0, 0)
    unpack(0)
    give_x(0).start()
    phase_two(0, 1)
    for copy in local_w:
        copy.wait()
    for copy in give_w:
        copy.wait_recv()
    give_x(0).wait_recv()
    ring_first(0)

    def start_second_group():
        phase_end(0, 1)
        unpack(1)
        give_x(1).start()
        give_x(1).wait_recv()
        ring_first(1)

    def gather_and_use(n, s):
        gather_round(n, s)
        second(n, s - 1)

    def events(n):
        rounds = [functools.partial(ring_round, n, s) for s in range(1, K)]
        rounds.append(functools.partial(activate, n))
        return rounds + [functools.partial(gather_and_use, n, s) for s in range(1, K + 1)]

    lead = 2
    first_events, second_events = events(0), [start_second_group] + events(1)
    for i in range(lead + len(second_events)):
        if i < len(first_events):
            first_events[i]()
        if i == len(first_events):
            way_back(0)
        if i >= lead:
            second_events[i - lead]()
    way_back(1)
    phase_two(1, 0)
    lax.fori_loop(0, NX // 2, weight_grads, 0)
    phase_two(1, 1)
    lax.fori_loop(NX // 2, NX, weight_grads, 0)

    sums = [None] * 3
    for n in range(2):
        phase_end(1, n)
        home = jnp.concatenate([flat_ra[1, n], flat_rb[1, n]], axis=1)
        for k in range(3):
            term = dot(qmat[n, k], home)
            sums[k] = term if n == 0 else sums[k] + term
    mixed[...] = (wcol[0] * sums[0] + wcol[1] * sums[1]).astype(BF)
    grad_tokens[...] = sums[2].astype(BF)

    for copy in give_w:
        copy.wait_send()
    for n in range(2):
        give_x(n).wait_send()
        for q in range(2):
            for d in order(NZ):
                p1a(q, n, d).wait_send()
                p2b(q, n, d).wait_send()
            for d in order(NY):
                p1b(q, n, d).wait_send()
                p2a(q, n, d).wait_send()
        for direction in range(2):
            for s in range(K):
                for q in range(2):
                    if exists(direction, s, q):
                        ring(n, direction, s, q).wait_send()
                    if ag_exists(direction, s, q):
                        ag(n, direction, s, q).wait_send()
        for args in crossed[n]:
            across(*args).wait_send()


def put_out(a, b, c, d, a_out, b_out, c_out, d_out, sem):
    pairs = ((c, c_out), (d, d_out), (a, a_out), (b, b_out))
    copies = [pltpu.make_async_copy(src, dst, sem.at[i]) for i, (src, dst) in enumerate(pairs)]
    for copy in copies:
        copy.start()
    for copy in copies:
        copy.wait()


def per_device(tokens, routes, route_weight, cotangent, w_in, w_out):
    T, F = tokens.shape
    E = lax.axis_size("expert")
    NX = lax.axis_size("dp") // 2
    NY = 1 << (int(math.log2(E)) // 2)
    NZ = E // NY
    U = w_out.shape[1]
    CAP = T * 2 * 5 // (4 * E)
    UB, K, HF, EG = U // NX, NX // 2, F // 2, E // 4
    dma = pltpu.SemaphoreType.DMA
    far = max(NZ, NY)
    vmem = pl.BlockSpec(memory_space=pltpu.VMEM)
    anywhere = pl.BlockSpec(memory_space=pl.ANY)

    def of_group(count):
        QR = EG * count
        return (
            pltpu.VMEM((2, 2, 2, QR, F), BF),
            pltpu.VMEM((2, 2, QR, F), BF),
            pltpu.VMEM((NX, 2, QR, 3 * UB), F32),
            pltpu.VMEM((2, K, 2, QR, 3 * UB), BF),
            pltpu.VMEM((2, K, 2, QR, 3 * UB), BF),
            pltpu.VMEM((NX, 2, 2, QR, 3 * UB), BF),
            pltpu.VMEM((2, 4 * QR, F), F32),
        )

    results = pl.pallas_call(
        functools.partial(kernel, NX, NZ, NY, CAP),
        out_shape=(
            jax.ShapeDtypeStruct((T, F), BF),
            jax.ShapeDtypeStruct((T, F), BF),
            jax.ShapeDtypeStruct((F, 2 * U), BF),
            jax.ShapeDtypeStruct((U, F), BF),
        ),
        in_specs=[pl.BlockSpec(memory_space=pltpu.HBM)] * 6,
        out_specs=(vmem,) * 4,
        scratch_shapes=[
            pltpu.VMEM((2, T), jnp.int32),
            pltpu.VMEM((2, T), F32),
            pltpu.VMEM((T, F), BF),
            pltpu.VMEM((T, F), BF),
            pltpu.VMEM((2, F, 2 * U), BF),
            pltpu.VMEM((2, U, F), BF),
            pltpu.VMEM((2, 2, NZ, NY, BLOCK, HF), BF),
            pltpu.VMEM((2, 2, NZ, NY, BLOCK, HF), BF),
            pltpu.VMEM((2, 2, NZ, NY, BLOCK, HF), BF),
            pltpu.VMEM((2, 2, NY, NZ, BLOCK, HF), BF),
            pltpu.VMEM((2, 2, NZ, NY, BLOCK, HF), BF),
            pltpu.VMEM((2, 2, NZ, NY, BLOCK, HF), BF),
            pltpu.VMEM((2, 3, T, E * BLOCK), BF),
            pltpu.VMEM((2, T, F), F32),
            *of_group((CAP + 1) // 2),
            *of_group(CAP // 2),
            dma((4,)), dma((2,)), dma((2,)), dma((2,)),
            dma((2, 2, 4, far)), dma((2, 2, 4, far)), dma((2, 2, 4)),
            dma((2,)), dma((2,)),
            dma((2, 2, K, 2)), dma((2, 2, K, 2)),
            dma((2, 2, K, 2)), dma((2, 2, K, 2)),
            dma((2, NX, 2)), dma((2, NX, 2)),
        ],
        compiler_params=pltpu.CompilerParams(
            collective_id=0, has_side_effects=True, vmem_limit_bytes=50 * 1024 * 1024
        ),
    )(
        *(
            pltpu.with_memory_space_constraint(v, pltpu.HBM)
            for v in (routes.T, route_weight.T, tokens, cotangent, w_in[0], w_out[0])
        )
    )
    mixed, grad_tokens, grad_in, grad_out = pl.pallas_call(
        put_out,
        out_shape=tuple(jax.ShapeDtypeStruct(r.shape, r.dtype) for r in results),
        in_specs=[anywhere] * 4,
        out_specs=(pl.BlockSpec(memory_space=pltpu.HBM),) * 4,
        scratch_shapes=[dma((4,))],
        compiler_params=pltpu.CompilerParams(vmem_limit_bytes=1024 * 1024),
    )(*results)
    return mixed, grad_tokens, grad_in[None], grad_out[None]


def solution(mesh):
    placed = (
        P("expert", "dp"),
        P("expert", None),
        P("expert", None),
        P("expert", "dp"),
        P("expert", "dp", None),
        P("expert", None, "dp"),
    )
    return jax.shard_map(
        per_device,
        mesh=mesh,
        in_specs=placed,
        out_specs=(
            P("expert", "dp"),
            P("expert", "dp"),
            P("expert", "dp", None),
            P("expert", None, "dp"),
        ),
        check_vma=False,
    )
```

time: 293 us -> 96.7 us (0.33)
  waiting for transfers between devices: 118 us -> 0 us
  Pallas kernels: 0 us -> 95.9 us
  starting transfers between devices: 57 us -> 0 us
  blocking collectives: 56.5 us -> 0 us
  local copies, waits for them, and re-layouts: 24.1 us -> 0 us
  matrix products: 15.7 us -> 0 us
  between operations: 15.6 us -> 0.64 us
  other arithmetic: 3.69 us -> 0 us
    pallas_call x0 -> x2, Pallas kernels: none -> 95.9 us  [the longest x1 94.7 us: per_device(): pl.pallas_call(functools.partial(kernel, NX, NZ, NY, CAP), out_shape=(jax...]
    unnamed x5 -> x0, waiting for transfers between devices: 85.9 us -> none
    all_to_all x4 -> x0, starting transfers between devices: 52.5 us -> none  [the longest x1 23.9 us: per_device(): lax.all_to_all(send_rows, 'expert', split_axis=0, concat_axis=0, tiled=True)]
    unnamed x1 -> x0, blocking collectives: 36.2 us -> none
    all_to_all x4 -> x0, waiting for transfers between devices: 32.5 us -> none  [the longest x1 11.7 us: per_device(): lax.all_to_all(out_rows.reshape(n_expert, local_experts * capacity, featu...]
    all_gather x1 -> x0, blocking collectives: 20.3 us -> none  [per_device(): lax.all_gather(hidden_share, 'dp', axis=0, tiled=True)]
    dot_general x10 -> x0, matrix products: 15.7 us -> none  [the longest x1 4.27 us: per_device(): jnp.einsum('secd,secf->edf', rows_four, both_four, preferred_element_type...]
    reshape x7 -> x0, local copies, waits for them, and re-layouts: 9.83 us -> none  [the longest x1 4.75 us: per_device(): pre_flat = pre_part.reshape(total_rows, 2 * hidden_units)]
  transfers between devices with their start and end apart: 8 -> 0, of which waited for: 6 -> 0; matrix products, arithmetic and copies ran while one was open for 22% -> 0% of each run, Pallas kernels for 0% -> 0%
where the time goes in v2:
time: 96.7 us; the launch traced here: 96.5 us
  Pallas kernels  95.9 us (99%)
    pallas_call x1, Pallas kernels, per_device(): pl.pallas_call(functools.partial(kernel, NX, NZ, NY, CAP), out_shape=(jax...  94.7 us

profile of v2, /device:TPU:1, one launch (start us, length us, event | category | flops | bytes accessed | tf_op | source)
XLA Modules:
  0.0 96.5 jit_solution(6658383532377068246)
XLA Ops:
  0.6 94.7 %shard_map.93 = (bf16[192,256]{1,0:T(8,128)(2,1)S(1)}, bf16[192,256]{1,0:T(8,128)(2,1)S(1)}, bf16[256,2048]{1,0:T(8,128)(2,1)S(1)}, bf16[1024,256]{1,0:T(8,128)(2,1)S(1)}) custom-call(s32[2,192]{1,0:T(2,128)} %bitcast.8, f32[2,192]{1,0:T(2,128)} %bitcast.9, bf16[192,256]{1,0:T(8,128)(2,1)} %tokens_h.1, bf16[192,256]{1,0:T(8,128)(2,1)} %cot_h.1, ...), custom_call_target="tpu_custom_call" | custom-call | tf_op jit(solution)/shard_map/pallas_call | solution.py:523
  95.3 1.2 %shard_map.94 = (bf16[192,256]{1,0:T(8,128)(2,1)}, bf16[192,256]{1,0:T(8,128)(2,1)}, bf16[256,2048]{1,0:T(8,128)(2,1)}, bf16[1024,256]{1,0:T(8,128)(2,1)}) custom-call(bf16[192,256]{1,0:T(8,128)(2,1)S(1)} %get-tuple-element.12.a, bf16[192,256]{1,0:T(8,128)(2,1)S(1)} %get-tuple-element.13.b, bf16[256,2048]{1,0:T(8,128)(2,1)S(1)} %get-tuple-element.14.c, ...), custom_call_target="tpu_custom_call" | custom-call | tf_op jit(solution)/shard_map/pallas_call | solution.py:566

commit v3 on v2

--- a/solution.py
+++ b/solution.py
@@ -395,58 +395,60 @@
     build(0)
     pl.semaphore_wait(barrier, NZ + NY + 1)
     phase_one(0, 0)
+    build(1)
+    phase_one(0, 1)
     give_w = [
         remote(w_in, wi.at[1], wsend.at[0], wrecv.at[0], partner),
         remote(w_out, wo.at[1], wsend.at[1], wrecv.at[1], partner),
     ]
     for copy in give_w:
         copy.start()
-    build(1)
-    phase_two(0, 0)
-    phase_one(0, 1)
     for k in range(2):
         wcol[k] = jnp.broadcast_to(wcols[k], (T, F))
+    phase_two(0, 0)
     ci = iota((T, E * BLOCK), 1)
     for n in range(2):
         for k in range(2):
             qmat[n, k] = ones_where(ci == cols_of[k][n])
         qmat[n, 2] = ones_where((ci == cols_of[0][n] + HALF) | (ci == cols_of[1][n] + HALF))
+    phase_two(0, 1)
     phase_end(0, 0)
     unpack(0)
     give_x(0).start()
-    phase_two(0, 1)
     for copy in local_w:
         copy.wait()
     for copy in give_w:
         copy.wait_recv()
     give_x(0).wait_recv()
     ring_first(0)
-
-    def start_second_group():
-        phase_end(0, 1)
-        unpack(1)
-        give_x(1).start()
-        give_x(1).wait_recv()
-        ring_first(1)
-
-    def gather_and_use(n, s):
-        gather_round(n, s)
-        second(n, s - 1)
-
-    def events(n):
-        rounds = [functools.partial(ring_round, n, s) for s in range(1, K)]
-        rounds.append(functools.partial(activate, n))
-        return rounds + [functools.partial(gather_and_use, n, s) for s in range(1, K + 1)]
-
-    lead = 2
-    first_events, second_events = events(0), [start_second_group] + events(1)
-    for i in range(lead + len(second_events)):
-        if i < len(first_events):
-            first_events[i]()
-        if i == len(first_events):
-            way_back(0)
-        if i >= lead:
-            second_events[i - lead]()
+    phase_end(0, 1)
+    unpack(1)
+    give_x(1).start()
+    ring_round(0, 1)
+    give_x(1).wait_recv()
+    ring_first(1)
+    for s in range(2, K):
+        ring_round(0, s)
+        ring_round(1, s - 1)
+    activate(0)
+    if K > 1:
+        ring_round(1, K - 1)
+    gather_round(0, 1)
+    activate(1)
+    second(0, 0)
+    for s in range(2, K):
+        gather_round(0, s)
+        second(0, s - 1)
+        gather_round(1, s - 1)
+        second(1, s - 2)
+    if K > 1:
+        gather_round(0, K)
+        second(0, K - 1)
+        gather_round(1, K - 1)
+        second(1, K - 2)
+    way_back(0)
+    gather_round(1, K)
+    second(1, K - 1)
     way_back(1)
     phase_two(1, 0)
     lax.fori_loop(0, NX // 2, weight_grads, 0)

time: 96.7 us -> 90.7 us (0.938)
  Pallas kernels: 95.9 us -> 89.9 us
    pallas_call x1, Pallas kernels: 94.7 us -> 88.7 us  [per_device(): pl.pallas_call(functools.partial(kernel, NX, NZ, NY, CAP), out_shape=(jax...]
where the time goes in v3:
time: 90.7 us; the launch traced here: 90.6 us
  Pallas kernels  89.9 us (99%)
    pallas_call x1, Pallas kernels, per_device(): pl.pallas_call(functools.partial(kernel, NX, NZ, NY, CAP), out_shape=(jax...  88.7 us

profile of v3, /device:TPU:1, one launch (start us, length us, event | category | flops | bytes accessed | tf_op | source)
XLA Modules:
  0.0 90.6 jit_solution(6432955737978367768)
XLA Ops:
  0.6 88.7 %shard_map.93 = (bf16[192,256]{1,0:T(8,128)(2,1)S(1)}, bf16[192,256]{1,0:T(8,128)(2,1)S(1)}, bf16[256,2048]{1,0:T(8,128)(2,1)S(1)}, bf16[1024,256]{1,0:T(8,128)(2,1)S(1)}) custom-call(s32[2,192]{1,0:T(2,128)} %bitcast.8, f32[2,192]{1,0:T(2,128)} %bitcast.9, bf16[192,256]{1,0:T(8,128)(2,1)} %tokens_h.1, bf16[192,256]{1,0:T(8,128)(2,1)} %cot_h.1, ...), custom_call_target="tpu_custom_call" | custom-call | tf_op jit(solution)/shard_map/pallas_call | solution.py:525
  89.3 1.2 %shard_map.94 = (bf16[192,256]{1,0:T(8,128)(2,1)}, bf16[192,256]{1,0:T(8,128)(2,1)}, bf16[256,2048]{1,0:T(8,128)(2,1)}, bf16[1024,256]{1,0:T(8,128)(2,1)}) custom-call(bf16[192,256]{1,0:T(8,128)(2,1)S(1)} %get-tuple-element.12.a, bf16[192,256]{1,0:T(8,128)(2,1)S(1)} %get-tuple-element.13.b, bf16[256,2048]{1,0:T(8,128)(2,1)S(1)} %get-tuple-element.14.c, ...), custom_call_target="tpu_custom_call" | custom-call | tf_op jit(solution)/shard_map/pallas_call | solution.py:568
